TPU v7x, 512 devices: a whole 4x8x8 slice. The times are simulated.
512 devices in a mesh: chan: 8 (over z), sx: 8 (over x, core), sy: 8 (over y).
Axes of the slice: x: 4, y: 8, z: 8, core: 2. Of those that a mesh axis runs over, the one named last changes fastest.
Arguments:
- volume: bfloat16 [8, 64, 64, 256], P('sx', 'sy', None, 'chan'), may hold values from -6 to 6
- kernel: bfloat16 [27, 256, 256], P(None, 'chan'), may hold values from -0.078125 to 0.078125
- grad_out: bfloat16 [8, 64, 64, 256], P('sx', 'sy', None, 'chan'), may hold values from -6 to 6
Outputs:
- out: bfloat16 [8, 64, 64, 256], P('sx', 'sy', None, 'chan')
- grad_input: bfloat16 [8, 64, 64, 256], P('sx', 'sy', None, 'chan')
- grad_kernel: float32 [27, 256, 256], P(None, 'chan')
All inputs are finite; a program needn't handle non-finite values.
Results may differ from a plain program's by a relative error of at most 0.0015.
Values may be sent and summed in bfloat16 or wider, within the bound.
No kernel may reach another device: no remote copies, remote signals or barrier semaphores. Data moves between devices by JAX's collectives and lax.ppermute only.
A program may use at most 64 MiB of HBM per device.

v0:
```python
import math
import jax
import jax.numpy as jnp
from jax import lax
from jax.sharding import PartitionSpec as P


def padded_2(shard, sides, width):
    for axis, dim in sides:
        count, length = (lax.axis_size(axis), shard.shape[dim])
        up = [(i, (i + 1) % count) for i in range(count - 1)]
        down = [(j, i) for i, j in up]
        last = lax.slice_in_dim(shard, length - width, length, axis=dim)
        leading = lax.slice_in_dim(shard, 0, width, axis=dim)
        before = lax.ppermute(last, axis, up)
        after = lax.ppermute(leading, axis, down)
        shard = jnp.concatenate([before, shard, after], axis=dim)
    return shard


def body(volume, kernel, grad_out):
    size_x, size_y, size_z, own_in = volume.shape
    total_out = kernel.shape[2]
    cells = size_x * size_y * size_z
    rim = padded_2(volume, (("sx", 0), ("sy", 1)), 1)
    padded = jnp.pad(rim, ((0, 0), (0, 0), (1, 1), (0, 0)))
    offsets = [(index // 9, index // 3 % 3, index % 3) for index in range(27)]
    partial_out = jnp.zeros((cells, total_out), jnp.float32)
    for index in range(27):
        a, b, e = offsets[index]
        window = padded[a : a + size_x, b : b + size_y, e : e + size_z].reshape(cells, own_in)
        partial_out = partial_out + jnp.dot(
            window, kernel[index], preferred_element_type=jnp.float32
        )
    partial_out = partial_out.reshape(size_x, size_y, size_z, total_out)
    out = lax.psum_scatter(partial_out, "chan", scatter_dimension=3, tiled=True).astype(
        jnp.bfloat16
    )
    grad_full = lax.all_gather(grad_out, "chan", axis=3, tiled=True)
    grad_rimmed = padded_2(grad_full, (("sx", 0), ("sy", 1)), 1)
    grad_padded = jnp.pad(grad_rimmed, ((0, 0), (0, 0), (1, 1), (0, 0)))
    flat_grad = grad_full.reshape(cells, total_out)
    back = jnp.zeros((cells, own_in), jnp.float32)
    kernel_terms = []
    for index in range(27):
        a, b, e = offsets[index]
        window = grad_padded[
            2 - a : 2 - a + size_x, 2 - b : 2 - b + size_y, 2 - e : 2 - e + size_z
        ].reshape(cells, total_out)
        back = back + lax.dot_general(
            window, kernel[index], (((1,), (1,)), ((), ())), preferred_element_type=jnp.float32
        )
        in_window = padded[a : a + size_x, b : b + size_y, e : e + size_z].reshape(cells, own_in)
        kernel_terms.append(
            lax.dot_general(
                in_window, flat_grad, (((0,), (0,)), ((), ())), preferred_element_type=jnp.float32
            )
        )
    grad_input = back.reshape(size_x, size_y, size_z, own_in).astype(jnp.bfloat16)
    local_kernel = jnp.stack(kernel_terms)
    summed = lax.psum(local_kernel, ("sx", "sy"))
    all_cells = cells * lax.axis_size("sx") * lax.axis_size("sy")
    grad_kernel = summed / jnp.float32(math.sqrt(all_cells))
    return (out, grad_input, grad_kernel)


def solution(mesh):
    return jax.shard_map(
        body,
        mesh=mesh,
        in_specs=(P("sx", "sy", None, "chan"), P(None, "chan", None), P("sx", "sy", None, "chan")),
        out_specs=(P("sx", "sy", None, "chan"), P("sx", "sy", None, "chan"), P(None, "chan", None)),
        check_vma=False,
    )
```

profile of v0, /device:TPU:25, one launch (start us, length us, event | category | flops | bytes accessed | tf_op | source)
XLA Modules:
  0.0 342.9 jit_solution(3898932481704692713)
XLA Ops:
  8.1 3.7 %collective-permute-start = (bf16[1,8,64,32]{2,3,1,0:T(8,128)(2,1)}, bf16[1,8,64,32]{2,3,1,0:T(8,128)(2,1)S(1)}, u32[]{:S(2)}, u32[]{:S(2)}) collective-permute-start(bf16[1,8,64,32]{2,3,1,0:T(8,128)(2,1)} %param.3), channel_id=1, source_target_pairs={{0,8},{8,16},{16,24},{24,32},{32,40},{40,48},{48,56},{1,9},{9,17},... | collective-permute-start | bytes 98312 | tf_op jit(solution)/shard_map/ppermute | solution.py:15
  11.7 1.9 collective-permute-start.1
  13.7 0.9 copy.98
  14.6 0.9 constant_dynamic-update-slice_fusion.1
  15.5 2.1 collective-permute-done.1
  17.6 2.1 collective-permute-start.3
  19.7 4.4 %collective-permute-start.2 = (bf16[3,1,64,32]{2,3,1,0:T(8,128)(2,1)S(1)}, bf16[3,1,64,32]{2,3,1,0:T(8,128)(2,1)S(1)}, u32[]{:S(2)}, u32[]{:S(2)}) collective-permute-start(bf16[3,1,64,32]{2,3,1,0:T(8,128)(2,1)S(1)} %get-tuple-element.68), channel_id=1, source_target_pairs={{0,1},{1,2},{2,3},{3,4},{4,5},{5,6},{6,7},{8,9},{9,10},{10,11},{11... | collective-permute-start | bytes 36872 | tf_op jit(solution)/shard_map/ppermute | solution.py:15
  24.1 26.2 %all_gather.3 = bf16[1,8,64,256]{2,1,0,3:T(8,128)(2,1)S(1)} all-gather(bf16[1,8,64,32]{2,1,0,3:T(8,128)(2,1)S(1)} %copy.98), channel_id=1, replica_groups=mesh['chan'=8,'sx'=8,'sy'=8] {'chan'}, dimensions={3}, use_global_device_ids=true | all-gather | bytes 294912 | tf_op jit(solution)/shard_map/all_gather | solution.py:39
  50.6 5.5 %collective-permute-start.5 = (bf16[1,8,64,256]{3,2,1,0:T(8,128)(2,1)S(1)}, bf16[1,8,64,256]{3,2,1,0:T(8,128)(2,1)S(1)}, u32[]{:S(2)}, u32[]{:S(2)}) collective-permute-start(bf16[1,8,64,256]{3,2,1,0:T(8,128)(2,1)S(1)} %copy.99), channel_id=1, source_target_pairs={{8,0},{16,8},{24,16},{32,24},{40,32},{48,40},{56,48},{9,1},{17,9},... | collective-permute-start | bytes 786440 | tf_op jit(solution)/shard_map/ppermute | solution.py:16
  56.1 4.7 %collective-permute-start.4 = (bf16[1,8,64,256]{3,2,1,0:T(8,128)(2,1)S(1)}, bf16[1,8,64,256]{3,2,1,0:T(8,128)(2,1)S(1)}, u32[]{:S(2)}, u32[]{:S(2)}) collective-permute-start(bf16[1,8,64,256]{3,2,1,0:T(8,128)(2,1)S(1)} %copy.99), channel_id=1, source_target_pairs={{0,8},{8,16},{16,24},{24,32},{32,40},{40,48},{48,56},{1,9},{9,17},... | collective-permute-start | bytes 786440 | tf_op jit(solution)/shard_map/ppermute | solution.py:15
  63.9 1.1 fusion.241
  65.0 0.8 fusion.37
  67.0 1.4 pad_maximum_fusion.13
  69.9 0.9 copy.72
  71.5 0.9 copy.73
  73.0 1.5 copy.76
  74.5 1.6 reshape.329
  76.1 1.5 copy.77
  77.6 1.6 reshape.330
  79.2 1.5 copy.78
  80.6 1.6 reshape.331
  82.2 1.5 copy.79
  83.7 1.6 reshape.332
  85.9 1.6 reshape.333
  88.1 1.6 reshape.334
  90.3 1.6 reshape.335
  91.9 1.5 copy.84
  93.4 1.6 reshape.337
  95.0 1.5 copy.85
  96.4 1.6 reshape.338
  98.7 1.6 reshape.339
  100.9 1.6 reshape.340
  102.4 1.5 copy.88
  103.9 1.6 reshape.341
  106.1 1.6 reshape.342
  107.7 1.5 copy.90
  109.2 1.6 reshape.343
  110.7 1.5 copy.91
  112.2 1.6 reshape.344
  114.5 1.6 reshape.347
  116.0 0.8 fusion.36
  116.8 0.9 fusion.35
  118.5 0.8 fusion.33
  119.3 0.9 fusion.32
  121.0 0.8 fusion.30
  121.9 0.9 fusion.29
  122.7 0.8 fusion.28
  123.6 0.8 fusion.27
  124.4 0.9 fusion.26
  126.1 0.8 fusion.24
  126.9 0.9 fusion.23
  127.8 0.8 fusion.22
  129.4 0.9 fusion.20
  131.9 0.9 fusion.17
  133.6 0.8 fusion.15
  134.4 0.9 fusion.14
  136.9 0.9 fusion.11
  146.8 1.9 collective-permute-start.7
  148.7 4.8 %collective-permute-start.6 = (bf16[3,1,64,256]{3,2,1,0:T(8,128)(2,1)S(1)}, bf16[3,1,64,256]{3,2,1,0:T(8,128)(2,1)S(1)}, u32[]{:S(2)}, u32[]{:S(2)}) collective-permute-start(bf16[3,1,64,256]{3,2,1,0:T(8,128)(2,1)S(1)} %get-tuple-element.39), channel_id=1, source_target_pairs={{0,1},{1,2},{2,3},{3,4},{4,5},{5,6},{6,7},{8,9},{9,10},{10,11},{11... | collective-permute-start | bytes 294920 | tf_op jit(solution)/shard_map/ppermute | solution.py:15
  153.8 1.3 copy.97
  155.8 0.9 fusion.240
  162.8 168.9 %all-reduce.4.cloned.1.call-done = f32[27,32,256]{2,1,0:T(8,128)} async-done(((f32[27,32,256]{2,1,0:T(8,128)}), f32[27,32,256]{2,1,0:T(8,128)}) %all-reduce.4.cloned.1.call-update) | async-done | bytes 884752 | tf_op jit(solution)/shard_map/psum | solution.py:61
  331.7 2.2 broadcast_multiply_fusion
  333.9 1.5 convert_element_type.21
  (189 shorter events, 34.9 us)
Async XLA Ops:
  8.0 52.8 %copy-start.4 = (bf16[1,8,64,32]{2,3,1,0:T(8,128)(2,1)S(1)}, bf16[1,8,64,32]{2,3,1,0:T(8,128)(2,1)}, u32[]{:S(2)}) copy-start(bf16[1,8,64,32]{2,3,1,0:T(8,128)(2,1)} %param.3) | copy-start | bytes 98308
  8.0 323.7 %all-reduce.4.cloned.1.call-start = ((), (), s32[]{:S(2)}) async-start(), calls=%async_computation.2 | async-start | bytes 1769472 | tf_op jit(solution)/shard_map/psum | solution.py:61
  8.1 6.5 %collective-permute-start = (bf16[1,8,64,32]{2,3,1,0:T(8,128)(2,1)}, bf16[1,8,64,32]{2,3,1,0:T(8,128)(2,1)S(1)}, u32[]{:S(2)}, u32[]{:S(2)}) collective-permute-start(bf16[1,8,64,32]{2,3,1,0:T(8,128)(2,1)} %param.3), channel_id=1, source_target_pairs={{0,8},{8,16},{16,24},{24,32},{32,40},{40,48},{48,56},{1,9},{9,17},... | collective-permute-start | bytes 98312 | tf_op jit(solution)/shard_map/ppermute | solution.py:15
  11.7 5.8 %collective-permute-start.1 = (bf16[1,8,64,32]{2,3,1,0:T(8,128)(2,1)}, bf16[1,8,64,32]{2,3,1,0:T(8,128)(2,1)S(1)}, u32[]{:S(2)}, u32[]{:S(2)}) collective-permute-start(bf16[1,8,64,32]{2,3,1,0:T(8,128)(2,1)} %param.3), channel_id=1, source_target_pairs={{8,0},{16,8},{24,16},{32,24},{40,32},{48,40},{56,48},{9,1},{17,9},... | collective-permute-start | bytes 98312 | tf_op jit(solution)/shard_map/ppermute | solution.py:16
  14.6 47.1 %copy-start.8 = (bf16[1,8,64,32]{2,3,1,0:T(8,128)(2,1)}, bf16[1,8,64,32]{2,3,1,0:T(8,128)(2,1)S(1)}, u32[]{:S(2)}) copy-start(bf16[1,8,64,32]{2,3,1,0:T(8,128)(2,1)S(1)} %collective-permute-done) | copy-start | bytes 98308
  17.5 45.0 %copy-start.6 = (bf16[1,8,64,32]{2,3,1,0:T(8,128)(2,1)}, bf16[1,8,64,32]{2,3,1,0:T(8,128)(2,1)S(1)}, u32[]{:S(2)}) copy-start(bf16[1,8,64,32]{2,3,1,0:T(8,128)(2,1)S(1)} %collective-permute-done.1) | copy-start | bytes 98308
  17.6 44.9 %collective-permute-start.3 = (bf16[3,1,64,32]{2,3,1,0:T(8,128)(2,1)S(1)}, bf16[3,1,64,32]{2,3,1,0:T(8,128)(2,1)S(1)}, u32[]{:S(2)}, u32[]{:S(2)}) collective-permute-start(bf16[3,1,64,32]{2,3,1,0:T(8,128)(2,1)S(1)} %get-tuple-element.69), channel_id=1, source_target_pairs={{1,0},{2,1},{3,2},{4,3},{5,4},{6,5},{7,6},{9,8},{10,9},{11,10},{12... | collective-permute-start | bytes 36872 | tf_op jit(solution)/shard_map/ppermute | solution.py:16
  19.7 42.9 %collective-permute-start.2 = (bf16[3,1,64,32]{2,3,1,0:T(8,128)(2,1)S(1)}, bf16[3,1,64,32]{2,3,1,0:T(8,128)(2,1)S(1)}, u32[]{:S(2)}, u32[]{:S(2)}) collective-permute-start(bf16[3,1,64,32]{2,3,1,0:T(8,128)(2,1)S(1)} %get-tuple-element.68), channel_id=1, source_target_pairs={{0,1},{1,2},{2,3},{3,4},{4,5},{5,6},{6,7},{8,9},{9,10},{10,11},{11... | collective-permute-start | bytes 36872 | tf_op jit(solution)/shard_map/ppermute | solution.py:15
  50.6 96.1 %collective-permute-start.5 = (bf16[1,8,64,256]{3,2,1,0:T(8,128)(2,1)S(1)}, bf16[1,8,64,256]{3,2,1,0:T(8,128)(2,1)S(1)}, u32[]{:S(2)}, u32[]{:S(2)}) collective-permute-start(bf16[1,8,64,256]{3,2,1,0:T(8,128)(2,1)S(1)} %copy.99), channel_id=1, source_target_pairs={{8,0},{16,8},{24,16},{32,24},{40,32},{48,40},{56,48},{9,1},{17,9},... | collective-permute-start | bytes 786440 | tf_op jit(solution)/shard_map/ppermute | solution.py:16
  56.1 90.7 %collective-permute-start.4 = (bf16[1,8,64,256]{3,2,1,0:T(8,128)(2,1)S(1)}, bf16[1,8,64,256]{3,2,1,0:T(8,128)(2,1)S(1)}, u32[]{:S(2)}, u32[]{:S(2)}) collective-permute-start(bf16[1,8,64,256]{3,2,1,0:T(8,128)(2,1)S(1)} %copy.99), channel_id=1, source_target_pairs={{0,8},{8,16},{16,24},{24,32},{32,40},{40,48},{48,56},{1,9},{9,17},... | collective-permute-start | bytes 786440 | tf_op jit(solution)/shard_map/ppermute | solution.py:15
  62.5 0.6 copy-start.36
  63.1 0.6 copy-start.37
  63.9 2.3 copy-start
  68.5 0.6 copy-start.2
  68.5 18.9 %copy-start.14 = (bf16[1,8,64,32]{2,3,1,0:T(8,128)(2,1)S(1)}, bf16[1,8,64,32]{2,3,1,0:T(8,128)(2,1)}, u32[]{:S(2)}) copy-start(bf16[1,8,64,32]{2,3,1,0:T(8,128)(2,1)} %get-tuple-element.51) | copy-start | bytes 98308
  68.5 21.2 %copy-start.13 = (bf16[1,8,64,32]{2,3,1,0:T(8,128)(2,1)S(1)}, bf16[1,8,64,32]{2,3,1,0:T(8,128)(2,1)}, u32[]{:S(2)}) copy-start(bf16[1,8,64,32]{2,3,1,0:T(8,128)(2,1)} %get-tuple-element.50) | copy-start | bytes 98308
  74.5 25.7 %copy-start.12 = (bf16[1,8,64,32]{2,3,1,0:T(8,128)(2,1)S(1)}, bf16[1,8,64,32]{2,3,1,0:T(8,128)(2,1)}, u32[]{:S(2)}) copy-start(bf16[1,8,64,32]{2,3,1,0:T(8,128)(2,1)} %get-tuple-element.47) | copy-start | bytes 98308
  88.1 25.7 %copy-start.11 = (bf16[1,8,64,32]{2,3,1,0:T(8,128)(2,1)S(1)}, bf16[1,8,64,32]{2,3,1,0:T(8,128)(2,1)}, u32[]{:S(2)}) copy-start(bf16[1,8,64,32]{2,3,1,0:T(8,128)(2,1)} %get-tuple-element.42) | copy-start | bytes 98308
  90.3 25.7 %copy-start.3 = (bf16[1,8,64,32]{2,3,1,0:T(8,128)(2,1)S(1)}, bf16[1,8,64,32]{2,3,1,0:T(8,128)(2,1)}, u32[]{:S(2)}) copy-start(bf16[1,8,64,32]{2,3,1,0:T(8,128)(2,1)} %copy-done.2) | copy-start | bytes 98308
  102.4 16.1 %copy-start.9 = (bf16[1,8,64,32]{2,3,1,0:T(8,128)(2,1)S(1)}, bf16[1,8,64,32]{2,3,1,0:T(8,128)(2,1)}, u32[]{:S(2)}) copy-start(bf16[1,8,64,32]{2,3,1,0:T(8,128)(2,1)} %copy-done.8) | copy-start | bytes 98308
  116.0 5.0 %copy-start.1 = (bf16[1,8,64,32]{2,3,1,0:T(8,128)(2,1)S(1)}, bf16[1,8,64,32]{2,3,1,0:T(8,128)(2,1)}, u32[]{:S(2)}) copy-start(bf16[1,8,64,32]{2,3,1,0:T(8,128)(2,1)} %get-tuple-element.60) | copy-start | bytes 98308
  121.0 5.0 %copy-start.5 = (bf16[1,8,64,32]{2,3,1,0:T(8,128)(2,1)S(1)}, bf16[1,8,64,32]{2,3,1,0:T(8,128)(2,1)}, u32[]{:S(2)}) copy-start(bf16[1,8,64,32]{2,3,1,0:T(8,128)(2,1)} %param.3) | copy-start | bytes 98308
  128.6 5.0 %copy-start.7 = (bf16[1,8,64,32]{2,3,1,0:T(8,128)(2,1)S(1)}, bf16[1,8,64,32]{2,3,1,0:T(8,128)(2,1)}, u32[]{:S(2)}) copy-start(bf16[1,8,64,32]{2,3,1,0:T(8,128)(2,1)} %copy-done.6) | copy-start | bytes 98308
  134.4 3.5 %copy-start.17 = (bf16[512,32]{0,1:T(8,128)(2,1)S(1)}, bf16[512,32]{0,1:T(8,128)(2,1)}, u32[]{:S(2)}) copy-start(bf16[512,32]{0,1:T(8,128)(2,1)} %reshape.324) | copy-start | bytes 98308
  136.9 1.2 copy-start.21
  137.8 0.8 copy-start.25
  137.8 196.1 %reduce-scatter.2.cloned.1.call-start = ((), (), s32[]{:S(2)}) async-start(), calls=%async_computation.1 | async-start | bytes 1179648 | tf_op jit(solution)/shard_map/reduce_scatter | solution.py:36
  138.2 0.8 copy-start.16
  138.6 0.8 copy-start.18
  138.9 0.8 copy-start.19
  139.3 0.8 copy-start.20
  139.7 0.8 copy-start.22
  140.1 0.8 copy-start.23
  140.4 0.8 copy-start.26
  140.9 0.8 copy-start.29
  141.2 0.8 copy-start.15
  141.6 0.8 copy-start.24
  142.0 0.8 copy-start.27
  142.4 0.8 copy-start.28
  142.7 0.8 copy-start.30
  143.2 0.8 copy-start.32
  143.5 0.8 copy-start.33
  143.9 0.8 copy-start.34
  144.3 0.8 copy-start.35
  145.0 0.8 copy-start.31
  145.8 0.8 copy-start.10
  146.8 8.3 %collective-permute-start.7 = (bf16[3,1,64,256]{3,2,1,0:T(8,128)(2,1)S(1)}, bf16[3,1,64,256]{3,2,1,0:T(8,128)(2,1)S(1)}, u32[]{:S(2)}, u32[]{:S(2)}) collective-permute-start(bf16[3,1,64,256]{3,2,1,0:T(8,128)(2,1)S(1)} %get-tuple-element.40), channel_id=1, source_target_pairs={{1,0},{2,1},{3,2},{4,3},{5,4},{6,5},{7,6},{9,8},{10,9},{11,10},{12... | collective-permute-start | bytes 294920 | tf_op jit(solution)/shard_map/ppermute | solution.py:16
  148.7 6.4 %collective-permute-start.6 = (bf16[3,1,64,256]{3,2,1,0:T(8,128)(2,1)S(1)}, bf16[3,1,64,256]{3,2,1,0:T(8,128)(2,1)S(1)}, u32[]{:S(2)}, u32[]{:S(2)}) collective-permute-start(bf16[3,1,64,256]{3,2,1,0:T(8,128)(2,1)S(1)} %get-tuple-element.39), channel_id=1, source_target_pairs={{0,1},{1,2},{2,3},{3,4},{4,5},{5,6},{6,7},{8,9},{9,10},{10,11},{11... | collective-permute-start | bytes 294920 | tf_op jit(solution)/shard_map/ppermute | solution.py:15
Sparse Core Ops, SparseCore 0:
  137.9 193.7 all-reduce.3
Sparse Core Ops, SparseCore 1:
  155.2 32.7 reduce-scatter.1
where the time goes:
time: 345 us; the launch traced here: 343 us
  waiting for transfers between devices  171 us (50%)
  local copies, waits for them, and re-layouts  60 us (17%)
  matrix products  34.2 us (10%)
  starting transfers between devices  29 us (8%)
  blocking collectives  26.2 us (8%)
  between operations  16.2 us (5%)
  other arithmetic  6.23 us (2%)
    psum x1, waiting for transfers between devices, body(): summed = lax.psum(local_kernel, ('sx', 'sy'))  169 us
    reshape x27, local copies, waits for them, and re-layouts, body(): padded[a:a + size_x, b:b + size_y, e:e + size_z].reshape(cells, own_in)  29.3 us
    all_gather x1, blocking collectives, body(): grad_full = lax.all_gather(grad_out, 'chan', axis=3, tiled=True)  26.2 us
    dot_general x27, matrix products, body(): lax.dot_general(in_window, flat_grad, (((0,), (0,)), ((), ())), preferred...  22.6 us
    slice x25, local copies, waits for them, and re-layouts, body(): padded[a:a + size_x, b:b + size_y, e:e + size_z].reshape(cells, own_in)  21 us
    ppermute x4, starting transfers between devices, padded_2(): before = lax.ppermute(last, axis, up)  17.6 us
    ppermute x4, starting transfers between devices, padded_2(): after = lax.ppermute(leading, axis, down)  11.4 us
    unnamed x81, local copies, waits for them, and re-layouts  6.98 us
  transfers between devices with their start and end apart: 10, of which 2 were waited for; matrix products, arithmetic and copies ran while one was open for 28% of the time, Pallas kernels for 0%

commit v1 on v0

--- a/solution.py
+++ b/solution.py
@@ -36,7 +36,13 @@
     out = lax.psum_scatter(partial_out, "chan", scatter_dimension=3, tiled=True).astype(
         jnp.bfloat16
     )
-    grad_full = lax.all_gather(grad_out, "chan", axis=3, tiled=True)
+    nodes = lax.axis_size("chan")
+    xs_all = []
+    for q in range(grad_out.ndim):
+        xs_all.append(nodes if q == 3 else 1)
+    grad_full = lax.all_to_all(
+        jnp.tile(grad_out, xs_all), axis_name="chan", split_axis=3, concat_axis=3, tiled=True
+    )
     grad_rimmed = padded_2(grad_full, (("sx", 0), ("sy", 1)), 1)
     grad_padded = jnp.pad(grad_rimmed, ((0, 0), (0, 0), (1, 1), (0, 0)))
     flat_grad = grad_full.reshape(cells, total_out)

time: 345 us -> 310 us (0.90)
  blocking collectives: 26.2 us -> 0 us
  matrix products: 34.2 us -> 17.5 us
  waiting for transfers between devices: 171 us -> 184 us
  local copies, waits for them, and re-layouts: 60 us -> 50.2 us
  starting transfers between devices: 29 us -> 34.4 us
    all_gather x1 -> x0, blocking collectives: 26.2 us -> none  [body(): grad_full = lax.all_gather(grad_out, 'chan', axis=3, tiled=True)]
    dot_general x27, matrix products: 22.6 us -> 5.83 us  [body(): lax.dot_general(in_window, flat_grad, (((0,), (0,)), ((), ())), preferred...]
    psum x1, waiting for transfers between devices: 169 us -> 180 us  [body(): summed = lax.psum(local_kernel, ('sx', 'sy'))]
    all_to_all x0 -> x1, starting transfers between devices: none -> 10 us  [body(): lax.all_to_all(jnp.tile(grad_out, xs_all), axis_name='chan', split_axis=3...]
    slice x25, local copies, waits for them, and re-layouts: 21 us -> 14.7 us  [body(): padded[a:a + size_x, b:b + size_y, e:e + size_z].reshape(cells, own_in)]
    reshape x27, local copies, waits for them, and re-layouts: 29.3 us -> 23.8 us  [body(): padded[a:a + size_x, b:b + size_y, e:e + size_z].reshape(cells, own_in)]
    ppermute x4, starting transfers between devices: 11.4 us -> 7.84 us  [padded_2(): after = lax.ppermute(leading, axis, down)]
    unnamed x81 -> x64, local copies, waits for them, and re-layouts: 6.98 us -> 7.61 us
  transfers between devices with their start and end apart: 10 -> 11, of which waited for: 2 -> 3; matrix products, arithmetic and copies ran while one was open for 28% -> 22% of each run, Pallas kernels for 0% -> 0%
where the time goes in v1:
time: 310 us; the launch traced here: 308 us
  waiting for transfers between devices  184 us (59%)
  local copies, waits for them, and re-layouts  50.2 us (16%)
  starting transfers between devices  34.4 us (11%)
  matrix products  17.5 us (6%)
  between operations  16.4 us (5%)
  other arithmetic  5.61 us (2%)
    psum x1, waiting for transfers between devices, body(): summed = lax.psum(local_kernel, ('sx', 'sy'))  180 us
    reshape x27, local copies, waits for them, and re-layouts, body(): padded[a:a + size_x, b:b + size_y, e:e + size_z].reshape(cells, own_in)  23.8 us
    ppermute x4, starting transfers between devices, padded_2(): before = lax.ppermute(last, axis, up)  16.5 us
    slice x25, local copies, waits for them, and re-layouts, body(): padded[a:a + size_x, b:b + size_y, e:e + size_z].reshape(cells, own_in)  14.7 us
    all_to_all x1, starting transfers between devices, body(): lax.all_to_all(jnp.tile(grad_out, xs_all), axis_name='chan', split_axis=3...  10 us
    ppermute x4, starting transfers between devices, padded_2(): after = lax.ppermute(leading, axis, down)  7.84 us
    unnamed x64, local copies, waits for them, and re-layouts  7.61 us
    dot_general x27, matrix products, body(): jnp.dot(window, kernel[index], preferred_element_type=jnp.float32)  6.65 us
  transfers between devices with their start and end apart: 11, of which 3 were waited for; matrix products, arithmetic and copies ran while one was open for 22% of the time, Pallas kernels for 0%

profile of v1, /device:TPU:25, one launch (start us, length us, event | category | flops | bytes accessed | tf_op | source)
XLA Modules:
  0.0 308.0 jit_solution(8132357685677638261)
XLA Ops:
  8.0 3.7 %collective-permute-start = (bf16[1,8,64,32]{2,3,1,0:T(8,128)(2,1)}, bf16[1,8,64,32]{2,3,1,0:T(8,128)(2,1)S(1)}, u32[]{:S(2)}, u32[]{:S(2)}) collective-permute-start(bf16[1,8,64,32]{2,3,1,0:T(8,128)(2,1)} %param.3), channel_id=1, source_target_pairs={{0,8},{8,16},{16,24},{24,32},{32,40},{40,48},{48,56},{1,9},{9,17},... | collective-permute-start | bytes 98312 | tf_op jit(solution)/shard_map/ppermute | solution.py:15
  11.7 1.9 collective-permute-start.1
  13.6 0.9 constant_dynamic-update-slice_fusion.1
  14.5 3.0 collective-permute-done.1
  17.5 2.1 collective-permute-start.3
  19.6 4.4 %collective-permute-start.2 = (bf16[3,1,64,32]{2,3,1,0:T(8,128)(2,1)S(1)}, bf16[3,1,64,32]{2,3,1,0:T(8,128)(2,1)S(1)}, u32[]{:S(2)}, u32[]{:S(2)}) collective-permute-start(bf16[3,1,64,32]{2,3,1,0:T(8,128)(2,1)S(1)} %get-tuple-element.68), channel_id=1, source_target_pairs={{0,1},{1,2},{2,3},{3,4},{4,5},{5,6},{6,7},{8,9},{9,10},{10,11},{11... | collective-permute-start | bytes 36872 | tf_op jit(solution)/shard_map/ppermute | solution.py:15
  24.0 0.9 tile.12
  25.0 0.3 copy.106
  25.3 1.1 reshape.439
  26.4 10.0 %all-to-all-start = ((bf16[8,2,8192]{2,1,0:T(2,128)(2,1)}), bf16[8,2,8192]{2,1,0:T(2,128)(2,1)S(1)}, u32[]{:S(2)}, u32[]{:S(2)}) async-start(bf16[8,2,8192]{2,1,0:T(2,128)(2,1)} %reshape.439), calls=%async_computation.1 | async-start | bytes 524288 | tf_op jit(solution)/shard_map/all_to_all | solution.py:43
  36.5 0.7 reshape.342
  37.3 0.7 reshape.333
  38.1 0.7 reshape.351
  38.8 0.6 copy-done.27
  39.4 0.6 copy-done.28
  40.2 1.0 fusion.241
  42.4 0.8 pad_maximum_fusion.13
  43.4 0.9 copy.72
  44.3 0.7 reshape.331
  45.0 0.9 copy.73
  45.9 0.7 reshape.332
  46.6 0.9 copy.76
  47.5 0.7 reshape.335
  48.2 0.7 copy.77
  48.9 1.6 reshape.336
  50.5 1.5 copy.78
  52.0 1.6 reshape.337
  53.6 0.6 copy.79
  54.2 1.6 reshape.338
  55.8 0.6 copy.80
  56.4 1.6 reshape.339
  58.0 1.5 copy.81
  59.5 1.6 reshape.340
  61.1 1.5 copy.82
  62.6 1.6 reshape.341
  64.1 1.5 copy.84
  65.6 1.6 reshape.343
  67.2 1.5 copy.85
  68.7 1.6 reshape.344
  70.2 0.7 copy.86
  70.9 1.6 reshape.345
  72.5 0.6 copy.87
  73.1 1.6 reshape.346
  74.7 0.7 reshape.347
  75.6 0.7 reshape.349
  76.4 0.7 reshape.350
  77.3 0.7 reshape.354
  86.2 0.3 reshape.440
  86.6 0.3 copy.99
  86.9 1.9 collective-permute-start.5
  88.8 3.6 %collective-permute-start.4 = (bf16[1,8,64,256]{3,2,1,0:T(8,128)(2,1)S(1)}, bf16[1,8,64,256]{3,2,1,0:T(8,128)(2,1)S(1)}, u32[]{:S(2)}, u32[]{:S(2)}) collective-permute-start(bf16[1,8,64,256]{3,2,1,0:T(8,128)(2,1)S(1)} %copy.99), channel_id=1, source_target_pairs={{0,8},{8,16},{16,24},{24,32},{32,40},{40,48},{48,56},{1,9},{9,17},... | collective-permute-start | bytes 786440 | tf_op jit(solution)/shard_map/ppermute | solution.py:15
  92.9 0.3 fusion.35
  93.5 0.3 fusion.32
  98.5 0.9 copy-done.1
  100.0 1.9 collective-permute-start.7
  101.9 4.8 %collective-permute-start.6 = (bf16[3,1,64,256]{3,2,1,0:T(8,128)(2,1)S(1)}, bf16[3,1,64,256]{3,2,1,0:T(8,128)(2,1)S(1)}, u32[]{:S(2)}, u32[]{:S(2)}) collective-permute-start(bf16[3,1,64,256]{3,2,1,0:T(8,128)(2,1)S(1)} %get-tuple-element.39), channel_id=1, source_target_pairs={{0,1},{1,2},{2,3},{3,4},{4,5},{5,6},{6,7},{8,9},{9,10},{10,11},{11... | collective-permute-start | bytes 294920 | tf_op jit(solution)/shard_map/ppermute | solution.py:15
  106.9 1.4 copy.97
  108.3 0.3 collective-permute-done.6
  108.6 0.6 select_maximum_fusion
  109.2 0.9 fusion.240
  115.6 0.6 copy.104
  116.3 180.5 %all-reduce.4.cloned.1.call-done = f32[27,32,256]{2,1,0:T(8,128)} async-done(((f32[27,32,256]{2,1,0:T(8,128)}), f32[27,32,256]{2,1,0:T(8,128)}) %all-reduce.4.cloned.1.call-update) | async-done | bytes 884752 | tf_op jit(solution)/shard_map/psum | solution.py:67
  296.8 2.2 broadcast_multiply_fusion
  299.0 1.5 convert_element_type.21
  (175 shorter events, 21.4 us)
Async XLA Ops:
  8.0 5.6 %collective-permute-start = (bf16[1,8,64,32]{2,3,1,0:T(8,128)(2,1)}, bf16[1,8,64,32]{2,3,1,0:T(8,128)(2,1)S(1)}, u32[]{:S(2)}, u32[]{:S(2)}) collective-permute-start(bf16[1,8,64,32]{2,3,1,0:T(8,128)(2,1)} %param.3), channel_id=1, source_target_pairs={{0,8},{8,16},{16,24},{24,32},{32,40},{40,48},{48,56},{1,9},{9,17},... | collective-permute-start | bytes 98312 | tf_op jit(solution)/shard_map/ppermute | solution.py:15
  11.7 5.8 %collective-permute-start.1 = (bf16[1,8,64,32]{2,3,1,0:T(8,128)(2,1)}, bf16[1,8,64,32]{2,3,1,0:T(8,128)(2,1)S(1)}, u32[]{:S(2)}, u32[]{:S(2)}) collective-permute-start(bf16[1,8,64,32]{2,3,1,0:T(8,128)(2,1)} %param.3), channel_id=1, source_target_pairs={{8,0},{16,8},{24,16},{32,24},{40,32},{48,40},{56,48},{9,1},{17,9},... | collective-permute-start | bytes 98312 | tf_op jit(solution)/shard_map/ppermute | solution.py:16
  17.5 21.3 %collective-permute-start.3 = (bf16[3,1,64,32]{2,3,1,0:T(8,128)(2,1)S(1)}, bf16[3,1,64,32]{2,3,1,0:T(8,128)(2,1)S(1)}, u32[]{:S(2)}, u32[]{:S(2)}) collective-permute-start(bf16[3,1,64,32]{2,3,1,0:T(8,128)(2,1)S(1)} %get-tuple-element.69), channel_id=1, source_target_pairs={{1,0},{2,1},{3,2},{4,3},{5,4},{6,5},{7,6},{9,8},{10,9},{11,10},{12... | collective-permute-start | bytes 36872 | tf_op jit(solution)/shard_map/ppermute | solution.py:16
  19.6 19.2 %collective-permute-start.2 = (bf16[3,1,64,32]{2,3,1,0:T(8,128)(2,1)S(1)}, bf16[3,1,64,32]{2,3,1,0:T(8,128)(2,1)S(1)}, u32[]{:S(2)}, u32[]{:S(2)}) collective-permute-start(bf16[3,1,64,32]{2,3,1,0:T(8,128)(2,1)S(1)} %get-tuple-element.68), channel_id=1, source_target_pairs={{0,1},{1,2},{2,3},{3,4},{4,5},{5,6},{6,7},{8,9},{9,10},{10,11},{11... | collective-permute-start | bytes 36872 | tf_op jit(solution)/shard_map/ppermute | solution.py:15
  24.9 11.5 %copy-start.2 = (bf16[1,8,64,32]{2,3,1,0:T(8,128)(2,1)S(1)}, bf16[1,8,64,32]{2,3,1,0:T(8,128)(2,1)}, u32[]{:S(2)}) copy-start(bf16[1,8,64,32]{2,3,1,0:T(8,128)(2,1)} %param.3) | copy-start | bytes 98308
  26.4 59.8 %all-to-all-start = ((bf16[8,2,8192]{2,1,0:T(2,128)(2,1)}), bf16[8,2,8192]{2,1,0:T(2,128)(2,1)S(1)}, u32[]{:S(2)}, u32[]{:S(2)}) async-start(bf16[8,2,8192]{2,1,0:T(2,128)(2,1)} %reshape.439), calls=%async_computation.1 | async-start | bytes 524288 | tf_op jit(solution)/shard_map/all_to_all | solution.py:43
  36.4 260.3 %all-reduce.4.cloned.1.call-start = ((), (), s32[]{:S(2)}) async-start(), calls=%async_computation.3 | async-start | bytes 1769472 | tf_op jit(solution)/shard_map/psum | solution.py:67
  38.8 0.6 copy-start.27
  39.4 0.6 copy-start.28
  40.1 1.4 copy-start
  43.3 10.3 %copy-start.6 = (bf16[1,8,64,32]{2,3,1,0:T(8,128)(2,1)S(1)}, bf16[1,8,64,32]{2,3,1,0:T(8,128)(2,1)}, u32[]{:S(2)}) copy-start(bf16[1,8,64,32]{2,3,1,0:T(8,128)(2,1)} %get-tuple-element.52) | copy-start | bytes 98308
  47.5 25.0 %copy-start.5 = (bf16[1,8,64,32]{2,3,1,0:T(8,128)(2,1)S(1)}, bf16[1,8,64,32]{2,3,1,0:T(8,128)(2,1)}, u32[]{:S(2)}) copy-start(bf16[1,8,64,32]{2,3,1,0:T(8,128)(2,1)} %get-tuple-element.47) | copy-start | bytes 98308
  48.9 25.8 %copy-start.4 = (bf16[1,8,64,32]{2,3,1,0:T(8,128)(2,1)S(1)}, bf16[1,8,64,32]{2,3,1,0:T(8,128)(2,1)}, u32[]{:S(2)}) copy-start(bf16[1,8,64,32]{2,3,1,0:T(8,128)(2,1)} %get-tuple-element.46) | copy-start | bytes 98308
  54.2 21.4 %copy-start.3 = (bf16[1,8,64,32]{2,3,1,0:T(8,128)(2,1)S(1)}, bf16[1,8,64,32]{2,3,1,0:T(8,128)(2,1)}, u32[]{:S(2)}) copy-start(bf16[1,8,64,32]{2,3,1,0:T(8,128)(2,1)} %get-tuple-element.45) | copy-start | bytes 98308
  75.5 2.9 copy-start.14
  78.1 0.8 copy-start.18
  78.3 0.8 copy-start.10
  78.8 0.8 copy-start.11
  79.1 0.8 copy-start.12
  79.6 0.8 copy-start.13
  79.9 0.8 copy-start.15
  80.3 0.8 copy-start.16
  80.6 0.8 copy-start.19
  81.1 0.8 copy-start.22
  81.4 0.8 copy-start.8
  81.9 0.8 copy-start.17
  82.1 0.8 copy-start.20
  82.6 0.8 copy-start.21
  82.9 0.8 copy-start.23
  83.4 0.8 copy-start.24
  84.2 0.8 copy-start.25
  84.4 0.8 copy-start.26
  84.9 0.8 copy-start.7
  86.9 13.0 %collective-permute-start.5 = (bf16[1,8,64,256]{3,2,1,0:T(8,128)(2,1)S(1)}, bf16[1,8,64,256]{3,2,1,0:T(8,128)(2,1)S(1)}, u32[]{:S(2)}, u32[]{:S(2)}) collective-permute-start(bf16[1,8,64,256]{3,2,1,0:T(8,128)(2,1)S(1)} %copy.99), channel_id=1, source_target_pairs={{8,0},{16,8},{24,16},{32,24},{40,32},{48,40},{56,48},{9,1},{17,9},... | collective-permute-start | bytes 786440 | tf_op jit(solution)/shard_map/ppermute | solution.py:16
  88.8 11.1 %collective-permute-start.4 = (bf16[1,8,64,256]{3,2,1,0:T(8,128)(2,1)S(1)}, bf16[1,8,64,256]{3,2,1,0:T(8,128)(2,1)S(1)}, u32[]{:S(2)}, u32[]{:S(2)}) collective-permute-start(bf16[1,8,64,256]{3,2,1,0:T(8,128)(2,1)S(1)} %copy.99), channel_id=1, source_target_pairs={{0,8},{8,16},{16,24},{24,32},{32,40},{40,48},{48,56},{1,9},{9,17},... | collective-permute-start | bytes 786440 | tf_op jit(solution)/shard_map/ppermute | solution.py:15
  97.6 1.9 copy-start.9
  98.5 0.9 copy-start.1
  99.4 199.5 %reduce-scatter.2.cloned.1.call-start = ((), (), s32[]{:S(2)}) async-start(), calls=%async_computation.2 | async-start | bytes 1179648 | tf_op jit(solution)/shard_map/reduce_scatter | solution.py:36
  100.0 8.3 %collective-permute-start.7 = (bf16[3,1,64,256]{3,2,1,0:T(8,128)(2,1)S(1)}, bf16[3,1,64,256]{3,2,1,0:T(8,128)(2,1)S(1)}, u32[]{:S(2)}, u32[]{:S(2)}) collective-permute-start(bf16[3,1,64,256]{3,2,1,0:T(8,128)(2,1)S(1)} %get-tuple-element.40), channel_id=1, source_target_pairs={{1,0},{2,1},{3,2},{4,3},{5,4},{6,5},{7,6},{9,8},{10,9},{11,10},{12... | collective-permute-start | bytes 294920 | tf_op jit(solution)/shard_map/ppermute | solution.py:16
  101.9 6.7 %collective-permute-start.6 = (bf16[3,1,64,256]{3,2,1,0:T(8,128)(2,1)S(1)}, bf16[3,1,64,256]{3,2,1,0:T(8,128)(2,1)S(1)}, u32[]{:S(2)}, u32[]{:S(2)}) collective-permute-start(bf16[3,1,64,256]{3,2,1,0:T(8,128)(2,1)S(1)} %get-tuple-element.39), channel_id=1, source_target_pairs={{0,1},{1,2},{2,3},{3,4},{4,5},{5,6},{6,7},{8,9},{9,10},{10,11},{11... | collective-permute-start | bytes 294920 | tf_op jit(solution)/shard_map/ppermute | solution.py:15
Sparse Core Ops, SparseCore 0:
  99.6 197.1 all-reduce.3
Sparse Core Ops, SparseCore 1:
  108.4 35.3 reduce-scatter.1
